TPU v7x, 32 devices: a whole 2x2x4 slice. The times are simulated.
32 devices in a mesh: space: 2 (over x), expert: 16 (over z, y, core).
Axes of the slice: x: 2, y: 2, z: 4, core: 2. Of those that a mesh axis runs over, the one named last changes fastest.
Arguments:
- vertex_tiles: bfloat16 [4096, 512], P(('space', 'expert')), may hold values from -6 to 6
- cotangent: bfloat16 [4096, 512], P(('space', 'expert')), may hold values from -3 to 3
- frames: int32 [4096], P(('space', 'expert')), may hold values from 0 to 5
- expert_ids: int32 [4096, 2], P(('space', 'expert')), may hold values from 0 to 15, as said below
- gate_values: bfloat16 [4096, 2], P(('space', 'expert')), may hold values from 0.19921875 to 1
- w_in: bfloat16 [16, 512, 4096], P('expert', None, 'space'), may hold values from -0.25 to 0.25
- w_out: bfloat16 [16, 4096, 512], P('expert', 'space'), may hold values from -0.09375 to 0.09375
Outputs:
- d_tiles: bfloat16 [4096, 512], P(('space', 'expert'))
- d_gates: bfloat16 [4096, 2], P(('space', 'expert'))
- d_w_in: float32 [16, 512, 4096], P('expert', None, 'space')
- d_w_out: float32 [16, 4096, 512], P('expert', 'space')
Inputs may be any that keep to these rules, and one draw needn't show every extreme that they name: `expert_ids`: in each device's aligned block of 128 tiles the two experts of a tile differ and no expert is named more than 20 times; one expert is named exactly 20 times in every block.
All inputs are finite; a program needn't handle non-finite values.
Results may differ from a plain program's by a relative error of at most 0.017.
Values may be sent and summed in bfloat16 or wider, within the bound.
A program may use at most 64 MiB of HBM per device.

v0:
```python
import math

import jax
import jax.numpy as jnp
from jax import lax
from jax.experimental import pallas as pl
from jax.experimental.pallas import tpu as pltpu
from jax.sharding import PartitionSpec as P


def rotation_tables(frames, half_width):
    pair_index = jnp.arange(half_width, dtype=jnp.int32)
    frequency = (1 + pair_index % 3).astype(jnp.float32)
    angles = frames.astype(jnp.float32)[:, None] * frequency[None, :] * (math.pi / 3.0)
    return (jnp.cos(angles), jnp.sin(angles))


def turn_forward(values, cos_table, sin_table):
    half_width = cos_table.shape[1]
    first_half = values[:, :half_width].astype(jnp.float32)
    second_half = values[:, half_width:].astype(jnp.float32)
    return jnp.concatenate(
        [
            cos_table * first_half - sin_table * second_half,
            sin_table * first_half + cos_table * second_half,
        ],
        axis=1,
    )


def turn_back(values, cos_table, sin_table):
    half_width = cos_table.shape[1]
    first_half = values[:, :half_width]
    second_half = values[:, half_width:]
    return jnp.concatenate(
        [
            cos_table * first_half + sin_table * second_half,
            cos_table * second_half - sin_table * first_half,
        ],
        axis=1,
    )


def gelu_pair(hidden):
    gelu_scale = math.sqrt(2.0 / math.pi)
    inner_arg = gelu_scale * (hidden + 0.044715 * hidden * hidden * hidden)
    tangent_h = jnp.tanh(inner_arg)
    activated = 0.5 * hidden * (1.0 + tangent_h)
    slope_term = 0.5 * (1.0 + tangent_h) + 0.5 * hidden * (
        1.0 - tangent_h * tangent_h
    ) * gelu_scale * (1.0 + 0.134145 * hidden * hidden)
    return (activated, slope_term)


def slot_targets(route_ids, capacity, expert_count):
    flat_ids = route_ids.reshape(-1)
    onehot = (flat_ids[:, None] == jnp.arange(expert_count, dtype=jnp.int32)[None, :]).astype(
        jnp.int32
    )
    slot_rank = jnp.sum(jnp.cumsum(onehot, axis=0) * onehot, axis=1) - 1
    return flat_ids * capacity + slot_rank


def fill_buffer(rows_x, rows_dy, gate_rows, targets, slots_total):
    positions = jnp.arange(slots_total, dtype=jnp.int32)
    matches = (positions[:, None] == targets[None, :]).astype(jnp.int32)
    filled = jnp.sum(matches, axis=1)
    source = jnp.sum(matches * jnp.arange(targets.shape[0], dtype=jnp.int32)[None, :], axis=1)
    token_index = source // 2
    occupied = filled > 0
    nothing = jnp.zeros((), jnp.bfloat16)
    buffer_x = jnp.where(occupied[:, None], jnp.take(rows_x, token_index, axis=0), nothing)
    buffer_dy = jnp.where(occupied[:, None], jnp.take(rows_dy, token_index, axis=0), nothing)
    buffer_g = jnp.where(occupied, jnp.take(gate_rows.reshape(-1), source, axis=0), nothing)
    return (buffer_x, buffer_dy, buffer_g)


def block_terms(rows_x, rows_dy, rows_g, first_weight, second_weight):
    hidden = jnp.dot(rows_x, first_weight, preferred_element_type=jnp.float32)
    activated, slope_term = gelu_pair(hidden)
    active = activated.astype(jnp.bfloat16)
    back = jnp.einsum("rd,fd->rf", rows_dy, second_weight, preferred_element_type=jnp.float32)
    gate_part = jnp.sum(back * active.astype(jnp.float32), axis=1)
    gate_col = rows_g.astype(jnp.float32)[:, None]
    scaled = (gate_col * rows_dy.astype(jnp.float32)).astype(jnp.bfloat16)
    pre = (gate_col * back * slope_term).astype(jnp.bfloat16)
    d_first = jnp.einsum("rd,rf->df", rows_x, pre, preferred_element_type=jnp.float32)
    d_second = jnp.einsum("rf,rd->fd", active, scaled, preferred_element_type=jnp.float32)
    row_part = jnp.einsum("rf,df->rd", pre, first_weight, preferred_element_type=jnp.float32)
    return (d_first, d_second, row_part, gate_part)


def run_blocks(blocks_x, blocks_dy, blocks_g, first_weight, second_weight):
    feature_dim = blocks_x.shape[2]

    def scan_step(carried, block_items):
        d_first, d_second, row_part, gate_part = block_terms(
            block_items[0], block_items[1], block_items[2], first_weight, second_weight
        )
        return ((carried[0] + d_first, carried[1] + d_second), (row_part, gate_part))

    start_value = (
        jnp.zeros(first_weight.shape, jnp.float32),
        jnp.zeros(second_weight.shape, jnp.float32),
    )
    sums, stacked = lax.scan(scan_step, start_value, (blocks_x, blocks_dy, blocks_g))
    return (sums[0], sums[1], stacked[0].reshape(-1, feature_dim), stacked[1].reshape(-1))


def on_device(vertex_tiles, cotangent, frames, expert_ids, gate_values, w_in, w_out):
    tile_count = vertex_tiles.shape[0]
    feature_dim = vertex_tiles.shape[1]
    expert_count = lax.axis_size("expert")
    space_count = lax.axis_size("space")
    capacity = 5 * tile_count // (2 * expert_count)
    slots_total = expert_count * capacity
    cos_table, sin_table = rotation_tables(frames, feature_dim // 2)
    rotated = turn_forward(vertex_tiles, cos_table, sin_table).astype(jnp.bfloat16)
    turned = turn_forward(cotangent, cos_table, sin_table).astype(jnp.bfloat16)
    first_weight = w_in[0]
    second_weight = w_out[0]
    own_targets = slot_targets(expert_ids, capacity, expert_count)
    group_x, group_dy, group_g = (
        lax.all_gather(rotated, "space", axis=0, tiled=True),
        lax.all_gather(turned, "space", axis=0, tiled=True),
        lax.all_gather(gate_values, "space", axis=0, tiled=True),
    )
    group_ids = lax.all_gather(expert_ids, "space", axis=0, tiled=True)

    def fill_group(rows_x, rows_dy, gate_rows, route_ids):
        return fill_buffer(
            rows_x, rows_dy, gate_rows, slot_targets(route_ids, capacity, expert_count), slots_total
        )

    buffer_x, buffer_dy, buffer_g = jax.vmap(fill_group)(
        group_x.reshape(space_count, tile_count, feature_dim),
        group_dy.reshape(space_count, tile_count, feature_dim),
        group_g.reshape(space_count, tile_count, 2),
        group_ids.reshape(space_count, tile_count, 2),
    )
    recv_x, recv_dy, recv_g = (
        lax.all_to_all(
            buffer_x.reshape(space_count, expert_count, capacity, feature_dim),
            "expert",
            split_axis=1,
            concat_axis=1,
            tiled=True,
        ),
        lax.all_to_all(
            buffer_dy.reshape(space_count, expert_count, capacity, feature_dim),
            "expert",
            split_axis=1,
            concat_axis=1,
            tiled=True,
        ),
        lax.all_to_all(
            buffer_g.reshape(space_count, expert_count, capacity),
            "expert",
            split_axis=1,
            concat_axis=1,
            tiled=True,
        ),
    )
    d_first, d_second, row_parts, gate_parts = run_blocks(
        recv_x.reshape(space_count, slots_total, feature_dim),
        recv_dy.reshape(space_count, slots_total, feature_dim),
        recv_g.reshape(space_count, slots_total),
        first_weight,
        second_weight,
    )
    summed_rows, summed_gates = (
        lax.psum_scatter(
            row_parts.astype(jnp.bfloat16), "space", scatter_dimension=0, tiled=True
        ).astype(jnp.float32),
        lax.psum_scatter(
            gate_parts.astype(jnp.bfloat16), "space", scatter_dimension=0, tiled=True
        ).astype(jnp.float32),
    )
    back_rows = summed_rows.astype(jnp.bfloat16).reshape(expert_count, capacity, feature_dim)
    back_gates = summed_gates.astype(jnp.bfloat16).reshape(expert_count, capacity)
    home_rows, home_gates = (
        lax.all_to_all(back_rows, "expert", split_axis=0, concat_axis=0, tiled=True),
        lax.all_to_all(back_gates, "expert", split_axis=0, concat_axis=0, tiled=True),
    )
    picked = jnp.take(home_rows.reshape(slots_total, feature_dim), own_targets, axis=0).astype(
        jnp.float32
    )
    picked = picked.reshape(tile_count, 2, feature_dim)
    total = picked[:, 0, :] + picked[:, 1, :]
    d_tiles = turn_back(total, cos_table, sin_table).astype(jnp.bfloat16)
    d_gates = jnp.take(home_gates.reshape(slots_total), own_targets, axis=0).reshape(tile_count, 2)
    return (d_tiles, d_gates, d_first[None], d_second[None])


MESH = pl.DeviceIdType.MESH
BF = jnp.bfloat16
F32 = jnp.float32
LEAD = 16
REST = 4
ORDER = (0, 1, 3, 2)


def mm(a, b, ca, cb):
    return lax.dot_general(a, b, (((ca,), (cb,)), ((), ())), preferred_element_type=F32)


def iota(shape, axis):
    return lax.broadcasted_iota(jnp.int32, shape, axis)


def by_quarter(quarter, pieces):
    low = jnp.where(quarter == 0, pieces[0], pieces[1])
    high = jnp.where(quarter == 2, pieces[2], pieces[3])
    return jnp.where(quarter < 2, low, high)


def fused(
    tiles_h, cotan_h, frames_h, ids_h, gates_h, w_in, w_out,
    d_tiles, d_gates, d_first, d_second,
    x_all, sc_all, act_all, pre_all,
    own_gate, far_gate, near_gate, out_gate, home_gate,
    send, recv, own_piece, far_piece, near_in, home_out, home, pick_m, pick_t, rows_acc,
    w1, w2, tiles, cotan, frames_t, ids_t, gates_t,
    sem_w, sem_self, s1, r1, s2, r2, s3, r3, s4, r4, s5, r5, s6, r6,
):
    space = lax.axis_index("space")
    me = lax.axis_index("expert")
    zed, low = me // 4, me % 4
    groups = lax.axis_size("expert") // 4
    slots = groups * 4
    other = 1 - space
    count, width = tiles_h.shape
    half = width // 2
    quarter_w = width // 4
    hidden_n = w1.shape[1]

    def dest(k, i):
        return lax.rem(zed - k + groups, groups) * 4 + lax.rem(low - i + 4, 4)

    def origin(k, i):
        return lax.rem(zed + k, groups) * 4 + lax.rem(low + i, 4)

    load1 = pltpu.make_async_copy(w_in.at[0], w1, sem_w.at[0])
    load2 = pltpu.make_async_copy(w_out.at[0], w2, sem_w.at[1])
    small = [
        pltpu.make_async_copy(src, dst, sem_w.at[2 + n])
        for n, (src, dst) in enumerate(
            (
                (ids_h, ids_t), (frames_h, frames_t), (gates_h, gates_t),
                (tiles_h, tiles), (cotan_h, cotan),
            )
        )
    ]
    for copy in small:
        copy.start()

    barrier = pltpu.get_barrier_semaphore()
    for s in range(1, slots):
        pl.semaphore_signal(
            barrier, inc=1, device_id=(space, dest(s // 4, s % 4)), device_id_type=MESH
        )
    pl.semaphore_signal(barrier, inc=1, device_id=(other, me), device_id_type=MESH)

    load1.start()
    load2.start()
    for copy in small:
        copy.wait()
    ids = ids_t[...]
    rel = lax.rem(zed - (ids >> 2) + groups, groups) * 4 + ((low - (ids & 3) + 4) & 3)
    upper = (iota((count, count), 0) < iota((count, count), 1)).astype(BF)
    hits = [(iota((slots, count), 0) == rel[k : k + 1, :]).astype(F32) for k in range(2)]
    before = mm(jnp.concatenate(hits, axis=0).astype(BF), upper, 1, 0)
    first_total = jnp.sum(hits[0], axis=1, keepdims=True)
    before = (before[:slots], before[slots:] + first_total)
    rows = slots * LEAD
    row_id = iota((rows, count), 0)
    row_tail = (row_id >> 4) * REST + (row_id & 3)
    ranks = []
    for k in range(2):
        rank = jnp.sum(before[k] * hits[k], axis=0, keepdims=True).astype(jnp.int32)
        ranks.append(rank)
        where = rel[k : k + 1, :]
        code_m = jnp.where(rank < LEAD, where * LEAD + rank, -1)
        code_t = jnp.where(rank >= LEAD, where * REST + rank - LEAD, -1)
        pick_m[k] = (row_id == code_m).astype(F32).astype(BF)
        pick_t[k] = (row_tail == code_t).astype(F32).astype(BF)

    diagonal = iota((count, count), 0) == iota((count, count), 1)
    frame = jnp.sum(jnp.where(diagonal, frames_t[...].astype(F32), 0.0), axis=1, keepdims=True)
    frequency = (1 + lax.rem(iota((1, half), 1), 3)).astype(F32)
    sixths = frequency * (frame - 6.0 * jnp.floor(frame * (1.0 / 6.0) + 0.01))
    sixths = sixths - 6.0 * jnp.floor(sixths * (1.0 / 6.0) + 0.01)
    folded = jnp.abs(sixths - 3.0)
    cos_v = jnp.where(
        folded > 2.5, 1.0, jnp.where(folded > 1.5, 0.5, jnp.where(folded > 0.5, -0.5, -1.0))
    )
    side = math.sqrt(3.0) / 2.0
    sin_v = jnp.where(
        (folded > 2.5) | (folded < 0.5), 0.0, jnp.where(sixths < 3.0, side, -side)
    )

    def turn(ref):
        u = ref[:, :half].astype(F32)
        v = ref[:, half:].astype(F32)
        return jnp.concatenate(
            [cos_v * u - sin_v * v, sin_v * u + cos_v * v], axis=1
        ).astype(BF)

    rotated = turn(tiles)
    turned = turn(cotan)
    g0 = gates_t[0:1, :].astype(F32)
    g1 = gates_t[1:2, :].astype(F32)

    def weighed(pick):
        return (pick[0].astype(F32) * g0 + pick[1].astype(F32) * g1).astype(BF)

    quarter = (iota((rows, 1), 0) >> 2) & 3
    send[:, :, 0:width] = (
        mm(pick_m[0] + pick_m[1], rotated, 1, 0).astype(BF).reshape(slots, LEAD, width)
    )
    send[:, :, width : 2 * width] = (
        mm(weighed(pick_m), turned, 1, 0).astype(BF).reshape(slots, LEAD, width)
    )
    tail_x = mm(pick_t[0] + pick_t[1], rotated, 1, 0)
    tail_y = mm(weighed(pick_t), turned, 1, 0)
    send[:, :, 2 * width :] = (
        by_quarter(
            quarter, (tail_x[:, :half], tail_x[:, half:], tail_y[:, :half], tail_y[:, half:])
        )
        .astype(BF)
        .reshape(slots, LEAD, half)
    )
    pl.semaphore_wait(barrier, slots)

    def remote(src, dst, a, b, who):
        return pltpu.make_async_remote_copy(
            src_ref=src, dst_ref=dst, send_sem=a, recv_sem=b, device_id=who, device_id_type=MESH
        )

    out_copy, relay_copy, piece_copy, home_copy = {}, {}, {}, {}
    piece_gate, home_gates = {}, {}
    self_copy = pltpu.make_async_copy(send.at[0], recv.at[0, 0], sem_self)
    self_copy.start()
    relay_copy[0] = remote(send.at[0], recv.at[1, 0], s2.at[0], r2.at[0], (other, me))
    relay_copy[0].start()
    for k in ORDER:
        for i in range(4):
            s = 4 * k + i
            if s:
                out_copy[s] = remote(
                    send.at[s], recv.at[0, s], s1.at[s], r1.at[s], (space, dest(k, i))
                )
                out_copy[s].start()

    block = 2 * 4 * LEAD
    rest = 2 * 4 * REST
    chunk = block + rest
    spread_q = (iota((block, 1), 0) >> 2) & 3
    tall_r = iota((block, rest), 0)
    grow = ((tall_r >> 4) * REST + (tall_r & 3) == iota((block, rest), 1)).astype(F32).astype(BF)
    flat_c = iota((rest, block), 1)
    same = (flat_c >> 4) * REST + (flat_c & 3) == iota((rest, block), 0)
    pulls = [
        (same & (((flat_c >> 2) & 3) == q)).astype(F32).astype(BF) for q in range(4)
    ]
    gelu_scale = math.sqrt(2.0 / math.pi)
    step_w = 512

    def arrive(k):
        for i in range(4):
            s = 4 * k + i
            if s:
                out_copy[s].wait_recv()
                relay_copy[s] = remote(
                    recv.at[0, s], recv.at[1, s], s2.at[s], r2.at[s], (other, me)
                )
                relay_copy[s].start()
            else:
                self_copy.wait()

    def work(k):
        for i in range(4):
            relay_copy[4 * k + i].wait_recv()
        base = k * chunk
        span = slice(4 * k, 4 * k + 4)
        x_all[base : base + block, :] = recv[:, span, :, 0:width].reshape(block, width)
        sc_all[base : base + block, :] = recv[:, span, :, width : 2 * width].reshape(block, width)
        tail = recv[:, span, :, 2 * width :].reshape(block, half)
        parts = [mm(pull, tail, 1, 0).astype(BF) for pull in pulls]
        x_all[base + block : base + chunk, :] = jnp.concatenate(parts[:2], axis=1)
        sc_all[base + block : base + chunk, :] = jnp.concatenate(parts[2:], axis=1)
        x_c = x_all[base : base + chunk, :]
        y_c = sc_all[base : base + chunk, :]
        rows_acc[...] = jnp.zeros_like(rows_acc)

        def tile(f, gate):
            cols = pl.ds(pl.multiple_of(f * step_w, step_w), step_w)
            w_a = w1[:, cols]
            h = mm(x_c, w_a, 1, 0)
            back = mm(y_c, w2[cols, :], 1, 1)
            sq = h * h
            t = jnp.tanh(gelu_scale * (h + 0.044715 * h * sq))
            up = 0.5 * (1.0 + t)
            active = (h * up).astype(BF)
            slope = up + 0.5 * h * (1.0 - t * t) * (gelu_scale + (gelu_scale * 0.134145) * sq)
            pre = (back * slope).astype(BF)
            act_all[base : base + chunk, cols] = active
            pre_all[base : base + chunk, cols] = pre
            rows_acc[...] += mm(pre, w_a, 1, 1)
            return gate + jnp.sum(back * active.astype(F32), axis=1, keepdims=True)

        gate = lax.fori_loop(0, hidden_n // step_w, tile, jnp.zeros((chunk, 1), F32))
        main = rows_acc[0:block, :].astype(BF)
        wide = mm(grow, rows_acc[block:chunk, :].astype(BF), 1, 0)
        packed = by_quarter(
            spread_q, [wide[:, q * quarter_w : (q + 1) * quarter_w] for q in range(4)]
        ).astype(BF)
        gate_b = jnp.broadcast_to(gate.astype(BF).astype(F32), (chunk, 128))
        lane = iota((block, 128), 1)
        gate_m = jnp.where(lane == (iota((block, 128), 0) & (LEAD - 1)), gate_b[:block], 0.0)
        lane = iota((rest, 128), 1)
        gate_r = jnp.where(
            lane == LEAD + (iota((rest, 128), 0) & (REST - 1)), gate_b[block:], 0.0
        )
        gates = jnp.sum(gate_m.reshape(8, LEAD, 128), axis=1) + jnp.sum(
            gate_r.reshape(8, REST, 128), axis=1
        )
        for i in range(4):
            own_gate[4 * k + i] = gates[i : i + 1]
            far_gate[4 * k + i] = gates[4 + i : 5 + i]
        both = jnp.concatenate([main, packed], axis=1).reshape(2, 4, LEAD, -1)
        far_piece[span] = both[1]
        own_piece[span] = both[0]
        piece_gate[k] = remote(
            far_gate.at[pl.ds(4 * k, 4)], near_gate.at[pl.ds(4 * k, 4)],
            s5.at[k], r5.at[k], (other, me),
        )
        piece_gate[k].start()
        for i in range(4):
            s = 4 * k + i
            piece_copy[s] = remote(
                far_piece.at[s], near_in.at[s], s3.at[s], r3.at[s], (other, me)
            )
            piece_copy[s].start()

    def finish(k):
        piece_gate[k].wait_recv()
        for i in range(4):
            s = 4 * k + i
            piece_copy[s].wait_recv()
            summed = (own_piece[s].astype(F32) + near_in[s].astype(F32)).astype(BF)
            gate = (own_gate[s] + near_gate[s]).astype(BF).astype(F32)
            if s:
                out_gate[s] = gate
                home_gates[s] = remote(
                    out_gate.at[s], home_gate.at[s], s6.at[s], r6.at[s], (space, origin(k, i))
                )
                home_gates[s].start()
                home_out[s] = summed
                home_copy[s] = remote(
                    home_out.at[s], home.at[s], s4.at[s], r4.at[s], (space, origin(k, i))
                )
                home_copy[s].start()
            else:
                home[s] = summed
                home_gate[s] = gate

    def first_tile(f, carry):
        cols = pl.ds(pl.multiple_of(f * step_w, step_w), step_w)
        d_first[:, cols] = mm(x_all[...], pre_all[:, cols], 0, 0)
        return carry

    def second_tile(f, carry):
        cols = pl.ds(pl.multiple_of(f * step_w, step_w), step_w)
        d_second[cols, :] = mm(act_all[:, cols], sc_all[...], 0, 0)
        return carry

    for n in range(len(ORDER) + 2):
        if n < len(ORDER):
            arrive(ORDER[n])
        if n == 1:
            load1.wait()
            load2.wait()
        if 1 <= n < len(ORDER) + 1:
            work(ORDER[n - 1])
        if n == len(ORDER):
            finish(ORDER[n - 2])
            lax.fori_loop(0, hidden_n // step_w, first_tile, 0)
        elif n >= 2:
            finish(ORDER[n - 2])
    lax.fori_loop(0, hidden_n // step_w, second_tile, 0)
    for s in range(1, slots):
        home_copy[s].wait_recv()
        home_gates[s].wait_recv()

    lead = home[:, :, 0:width].reshape(rows, width)
    packed = home[:, :, width : width + quarter_w].reshape(rows, quarter_w)
    nothing = jnp.zeros((), BF)
    spread = jnp.concatenate([jnp.where(quarter == q, packed, nothing) for q in range(4)], axis=1)
    total = mm(pick_m[0] + pick_m[1], lead, 0, 0) + mm(pick_t[0] + pick_t[1], spread, 0, 0)
    a, b = total[:, :half], total[:, half:]
    d_tiles[...] = jnp.concatenate(
        [cos_v * a + sin_v * b, cos_v * b - sin_v * a], axis=1
    ).astype(BF)
    gate_rows = home_gate[...].reshape(slots, 128).astype(BF)
    for k in range(2):
        got = mm(gate_rows, hits[k].astype(BF), 0, 0)
        row = jnp.sum(jnp.where(iota((128, count), 0) == ranks[k], got, 0.0), axis=0, keepdims=True)
        d_gates[k : k + 1, :] = (row / gates_t[k : k + 1, :].astype(F32)).astype(BF)

    for s in range(slots):
        if s:
            out_copy[s].wait_send()
            home_copy[s].wait_send()
            home_gates[s].wait_send()
        relay_copy[s].wait_send()
        piece_copy[s].wait_send()
    for k in ORDER:
        piece_gate[k].wait_send()


def write_out(*refs):
    held, outs, sem = refs[:4], refs[4:8], refs[8]
    copies = [pltpu.make_async_copy(held[n], outs[n], sem.at[n]) for n in range(4)]
    for copy in copies:
        copy.start()
    for copy in copies:
        copy.wait()


def on_device_fused(vertex_tiles, cotangent, frames, expert_ids, gate_values, w_in, w_out):
    count, width = vertex_tiles.shape
    hidden_n = w_in.shape[2]
    slots = lax.axis_size("expert")
    rows = 2 * slots * (LEAD + REST)
    block_w = 2 * width + width // 2
    piece_w = width + width // 4
    vmem = pl.BlockSpec(memory_space=pltpu.VMEM)
    hbm = pl.BlockSpec(memory_space=pltpu.HBM)
    dma = pltpu.SemaphoreType.DMA
    shape = jax.ShapeDtypeStruct
    row = pltpu.VMEM((slots, 1, 128), F32)
    d_tiles, d_gates, d_first, d_second = pl.pallas_call(
        fused,
        out_shape=(
            shape((count, width), BF),
            shape((2, count), BF),
            shape((width, hidden_n), F32),
            shape((hidden_n, width), F32),
        ),
        in_specs=[hbm] * 7,
        out_specs=[vmem] * 4,
        scratch_shapes=[
            pltpu.VMEM((rows, width), BF),
            pltpu.VMEM((rows, width), BF),
            pltpu.VMEM((rows, hidden_n), BF),
            pltpu.VMEM((rows, hidden_n), BF),
            row, row, row, row, row,
            pltpu.VMEM((slots, LEAD, block_w), BF),
            pltpu.VMEM((2, slots, LEAD, block_w), BF),
            pltpu.VMEM((slots, LEAD, piece_w), BF),
            pltpu.VMEM((slots, LEAD, piece_w), BF),
            pltpu.VMEM((slots, LEAD, piece_w), BF),
            pltpu.VMEM((slots, LEAD, piece_w), BF),
            pltpu.VMEM((slots, LEAD, piece_w), BF),
            pltpu.VMEM((2, slots * LEAD, count), BF),
            pltpu.VMEM((2, slots * LEAD, count), BF),
            pltpu.VMEM((8 * (LEAD + REST), width), F32),
            pltpu.VMEM((width, hidden_n), BF),
            pltpu.VMEM((hidden_n, width), BF),
            pltpu.VMEM((count, width), BF),
            pltpu.VMEM((count, width), BF),
            pltpu.VMEM((1, count), jnp.int32),
            pltpu.VMEM((2, count), jnp.int32),
            pltpu.VMEM((2, count), BF),
            dma((7,)),
            dma(()),
        ]
        + [dma((slots,))] * 12,
        compiler_params=pltpu.CompilerParams(
            collective_id=0, has_side_effects=True, vmem_limit_bytes=36 * 1024 * 1024
        ),
    )(
        *[
            pltpu.with_memory_space_constraint(a, pltpu.HBM)
            for a in (
                vertex_tiles, cotangent, frames[None], expert_ids.T, gate_values.T, w_in, w_out
            )
        ]
    )
    results = (d_tiles, d_gates, d_first, d_second)
    d_tiles, d_gates, d_first, d_second = pl.pallas_call(
        write_out,
        out_shape=tuple(shape(a.shape, a.dtype) for a in results),
        in_specs=[vmem] * 4,
        out_specs=[hbm] * 4,
        scratch_shapes=[dma((4,))],
        compiler_params=pltpu.CompilerParams(vmem_limit_bytes=4 * 1024 * 1024),
    )(*results)
    return (d_tiles, d_gates.T, d_first[None], d_second[None])


def fits(mesh):
    return mesh.shape["space"] == 2 and mesh.shape["expert"] == 16


def solution(mesh):
    in_specs = (
        P(("space", "expert"), None),
        P(("space", "expert"), None),
        P(("space", "expert")),
        P(("space", "expert"), None),
        P(("space", "expert"), None),
        P("expert", None, "space"),
        P("expert", "space", None),
    )
    out_specs = (
        P(("space", "expert"), None),
        P(("space", "expert"), None),
        P("expert", None, "space"),
        P("expert", "space", None),
    )
    return jax.shard_map(
        on_device_fused if fits(mesh) else on_device, mesh=mesh, in_specs=in_specs, out_specs=out_specs, check_vma=False
    )
```

profile of v0, /device:TPU:1, one launch (start us, length us, event | category | flops | bytes accessed | tf_op | source)
XLA Modules:
  0.0 46.7 jit_solution(13713018172635339637)
XLA Ops:
  0.6 42.6 %shard_map.102 = (bf16[128,512]{1,0:T(8,128)(2,1)S(1)}, bf16[2,128]{1,0:T(2,128)(2,1)S(1)}, f32[512,2048]{1,0:T(8,128)S(1)}, f32[2048,512]{1,0:T(8,128)S(1)}) custom-call(bf16[128,512]{1,0:T(8,128)(2,1)} %tiles_h.1, bf16[128,512]{1,0:T(8,128)(2,1)} %cotan_h.1, s32[1,128]{1,0:T(1,128)} %bitcast.7, s32[2,128]{1,0:T(2,128)} %bitcast.6, bf16[2,128]{1,0:T(2,128)(2,1)} %bitcast.8, ...), custom_call_target="tpu_custom_call" | custom-call | tf_op jit(solution)/shard_map/pallas_call | solution.py:543
  43.3 3.5 %shard_map.103 = (bf16[128,512]{1,0:T(8,128)(2,1)}, bf16[2,128]{1,0:T(2,128)(2,1)}, f32[512,2048]{1,0:T(8,128)}, f32[2048,512]{1,0:T(8,128)}) custom-call(bf16[128,512]{1,0:T(8,128)(2,1)S(1)} %get-tuple-element.12.refs_0_, bf16[2,128]{1,0:T(2,128)(2,1)S(1)} %get-tuple-element.13.refs_1_, f32[512,2048]{1,0:T(8,128)S(1)} %get-tuple-element.14.refs_2_, ...), custom_call_target="tpu_custom_call" | custom-call | tf_op jit(solution)/shard_map/pallas_call | solution.py:592
where the time goes:
time: 47.3 us; the launch traced here: 46.7 us
  Pallas kernels  46.1 us (97%)
  between operations  0.64 us (1%)
    pallas_call x1, Pallas kernels, on_device_fused(): pl.pallas_call(fused, out_shape=(shape((count, width), BF), shape((2, cou...  42.6 us
    pallas_call x1, Pallas kernels, on_device_fused(): pl.pallas_call(write_out, out_shape=tuple((shape(a.shape, a.dtype) for a...  3.48 us

commit v1 on v0

--- a/solution.py
+++ b/solution.py
@@ -1,3 +1,4 @@
+import contextlib
 import math
 
 import jax
@@ -197,7 +198,16 @@
 F32 = jnp.float32
 LEAD = 16
 REST = 4
-ORDER = (0, 1, 3, 2)
+SELF = 12
+CHUNKS = ((0, 4), (4, 8), (8, 12), (12, 16))
+DIRECT = 8
+SENDS = (13, 14, 15, 0, 1, 2, 3, 4, 5, 6, 7, 8, 9, 10, 11)
+FIRST = (13, 14, 0, 1, 2, 3, 15, 4)
+DURING = ((6, 5, 7), (8, 9, 10, 11), (), ())
+
+
+def mark(name):
+    return contextlib.nullcontext()
 
 
 def mm(a, b, ca, cb):
@@ -226,19 +236,22 @@
     space = lax.axis_index("space")
     me = lax.axis_index("expert")
     zed, low = me // 4, me % 4
-    groups = lax.axis_size("expert") // 4
-    slots = groups * 4
+    slots = lax.axis_size("expert")
     other = 1 - space
     count, width = tiles_h.shape
     half = width // 2
     quarter_w = width // 4
     hidden_n = w1.shape[1]
 
-    def dest(k, i):
-        return lax.rem(zed - k + groups, groups) * 4 + lax.rem(low - i + 4, 4)
-
-    def origin(k, i):
-        return lax.rem(zed + k, groups) * 4 + lax.rem(low + i, 4)
+    def flip(value, bits):
+        if bits == 1:
+            return value + 1 - 2 * lax.rem(value, 2)
+        return (value, value, lax.rem(value + 2, 4), 3 - value)[bits]
+
+    def peer(s):
+        if s >= SELF:
+            return flip(zed, 0) * 4 + flip(low, s - SELF)
+        return flip(zed, (1, 3, 2)[s % 3]) * 4 + flip(low, s // 3)
 
     load1 = pltpu.make_async_copy(w_in.at[0], w1, sem_w.at[0])
     load2 = pltpu.make_async_copy(w_out.at[0], w2, sem_w.at[1])
@@ -255,18 +268,23 @@
         copy.start()
 
     barrier = pltpu.get_barrier_semaphore()
-    for s in range(1, slots):
+    peers = [s for s in range(slots) if s != SELF]
+    for s in peers:
+        pl.semaphore_signal(barrier, inc=1, device_id=(space, peer(s)), device_id_type=MESH)
+    for s in range(DIRECT, slots):
         pl.semaphore_signal(
-            barrier, inc=1, device_id=(space, dest(s // 4, s % 4)), device_id_type=MESH
-        )
-    pl.semaphore_signal(barrier, inc=1, device_id=(other, me), device_id_type=MESH)
+            barrier, inc=1, device_id=(other, peer(s)), device_id_type=MESH
+        )
 
     load1.start()
     load2.start()
-    for copy in small:
-        copy.wait()
+    with mark("small"):
+        for copy in small:
+            copy.wait()
     ids = ids_t[...]
-    rel = lax.rem(zed - (ids >> 2) + groups, groups) * 4 + ((low - (ids & 3) + 4) & 3)
+    rel = ids ^ me
+    near, plane = rel & 3, (rel >> 2) ^ (rel >> 3)
+    rel = jnp.where(plane == 0, SELF + near, 3 * near + plane - 1)
     upper = (iota((count, count), 0) < iota((count, count), 1)).astype(BF)
     hits = [(iota((slots, count), 0) == rel[k : k + 1, :]).astype(F32) for k in range(2)]
     before = mm(jnp.concatenate(hits, axis=0).astype(BF), upper, 1, 0)
@@ -330,7 +348,8 @@
         .astype(BF)
         .reshape(slots, LEAD, half)
     )
-    pl.semaphore_wait(barrier, slots)
+    with mark("barrier_wait"):
+        pl.semaphore_wait(barrier, 2 * slots - 1 - DIRECT)
 
     def remote(src, dst, a, b, who):
         return pltpu.make_async_remote_copy(
@@ -338,51 +357,53 @@
         )
 
     out_copy, relay_copy, piece_copy, home_copy = {}, {}, {}, {}
-    piece_gate, home_gates = {}, {}
-    self_copy = pltpu.make_async_copy(send.at[0], recv.at[0, 0], sem_self)
+    piece_gate, home_gates, far_gates = {}, {}, {}
+    self_copy = pltpu.make_async_copy(send.at[SELF], recv.at[0, SELF], sem_self)
     self_copy.start()
-    relay_copy[0] = remote(send.at[0], recv.at[1, 0], s2.at[0], r2.at[0], (other, me))
-    relay_copy[0].start()
-    for k in ORDER:
-        for i in range(4):
-            s = 4 * k + i
-            if s:
-                out_copy[s] = remote(
-                    send.at[s], recv.at[0, s], s1.at[s], r1.at[s], (space, dest(k, i))
-                )
-                out_copy[s].start()
-
-    block = 2 * 4 * LEAD
-    rest = 2 * 4 * REST
-    chunk = block + rest
-    spread_q = (iota((block, 1), 0) >> 2) & 3
-    tall_r = iota((block, rest), 0)
-    grow = ((tall_r >> 4) * REST + (tall_r & 3) == iota((block, rest), 1)).astype(F32).astype(BF)
-    flat_c = iota((rest, block), 1)
-    same = (flat_c >> 4) * REST + (flat_c & 3) == iota((rest, block), 0)
-    pulls = [
-        (same & (((flat_c >> 2) & 3) == q)).astype(F32).astype(BF) for q in range(4)
-    ]
+    relay_copy[SELF] = remote(
+        send.at[SELF], recv.at[1, SELF], s2.at[SELF], r2.at[SELF], (other, me)
+    )
+    relay_copy[SELF].start()
+    for s in SENDS:
+        out_copy[s] = remote(send.at[s], recv.at[0, s], s1.at[s], r1.at[s], (space, peer(s)))
+        out_copy[s].start()
+
+    consts = {}
+    for lo, hi in CHUNKS:
+        block, rest = 2 * (hi - lo) * LEAD, 2 * (hi - lo) * REST
+        if block in consts:
+            continue
+        spread_q = (iota((block, 1), 0) >> 2) & 3
+        tall_r = iota((block, rest), 0)
+        grow = (tall_r >> 4) * REST + (tall_r & 3) == iota((block, rest), 1)
+        flat_c = iota((rest, block), 1)
+        same = (flat_c >> 4) * REST + (flat_c & 3) == iota((rest, block), 0)
+        pulls = [
+            (same & (((flat_c >> 2) & 3) == q)).astype(F32).astype(BF) for q in range(4)
+        ]
+        consts[block] = (spread_q, grow.astype(F32).astype(BF), pulls)
     gelu_scale = math.sqrt(2.0 / math.pi)
     step_w = 512
 
-    def arrive(k):
-        for i in range(4):
-            s = 4 * k + i
-            if s:
-                out_copy[s].wait_recv()
-                relay_copy[s] = remote(
-                    recv.at[0, s], recv.at[1, s], s2.at[s], r2.at[s], (other, me)
-                )
-                relay_copy[s].start()
-            else:
-                self_copy.wait()
-
-    def work(k):
-        for i in range(4):
-            relay_copy[4 * k + i].wait_recv()
-        base = k * chunk
-        span = slice(4 * k, 4 * k + 4)
+    def relay(s):
+        with mark("arrive%d" % s):
+            out_copy[s].wait_recv()
+        relay_copy[s] = remote(
+            recv.at[0, s], recv.at[1, s], s2.at[s], r2.at[s], (other, me)
+        )
+        relay_copy[s].start()
+
+    def work(c):
+        lo, hi = CHUNKS[c]
+        n = hi - lo
+        block, rest = 2 * n * LEAD, 2 * n * REST
+        chunk = block + rest
+        spread_q, grow, pulls = consts[block]
+        with mark("relayed%d" % c):
+            for s in range(lo, hi):
+                relay_copy[s].wait_recv()
+        base = 2 * lo * (LEAD + REST)
+        span = slice(lo, hi)
         x_all[base : base + block, :] = recv[:, span, :, 0:width].reshape(block, width)
         sc_all[base : base + block, :] = recv[:, span, :, width : 2 * width].reshape(block, width)
         tail = recv[:, span, :, 2 * width :].reshape(block, half)
@@ -391,10 +412,11 @@
         sc_all[base + block : base + chunk, :] = jnp.concatenate(parts[2:], axis=1)
         x_c = x_all[base : base + chunk, :]
         y_c = sc_all[base : base + chunk, :]
-        rows_acc[...] = jnp.zeros_like(rows_acc)
+        acc = rows_acc.at[0:chunk]
+        acc[...] = jnp.zeros((chunk, width), F32)
 
         def tile(f, gate):
-            cols = pl.ds(pl.multiple_of(f * step_w, step_w), step_w)
+            cols = pl.ds(f * step_w, step_w)
             w_a = w1[:, cols]
             h = mm(x_c, w_a, 1, 0)
             back = mm(y_c, w2[cols, :], 1, 1)
@@ -406,10 +428,14 @@
             pre = (back * slope).astype(BF)
             act_all[base : base + chunk, cols] = active
             pre_all[base : base + chunk, cols] = pre
-            rows_acc[...] += mm(pre, w_a, 1, 1)
+            acc[...] += mm(pre, w_a, 1, 1)
             return gate + jnp.sum(back * active.astype(F32), axis=1, keepdims=True)
 
-        gate = lax.fori_loop(0, hidden_n // step_w, tile, jnp.zeros((chunk, 1), F32))
+        gate = jnp.zeros((chunk, 1), F32)
+        for f in range(hidden_n // step_w):
+            gate = tile(f, gate)
+            for s in DURING[c][f : f + 1] if f < hidden_n // step_w - 1 else DURING[c][f:]:
+                relay(s)
         main = rows_acc[0:block, :].astype(BF)
         wide = mm(grow, rows_acc[block:chunk, :].astype(BF), 1, 0)
         packed = by_quarter(
@@ -422,76 +448,96 @@
         gate_r = jnp.where(
             lane == LEAD + (iota((rest, 128), 0) & (REST - 1)), gate_b[block:], 0.0
         )
-        gates = jnp.sum(gate_m.reshape(8, LEAD, 128), axis=1) + jnp.sum(
-            gate_r.reshape(8, REST, 128), axis=1
-        )
-        for i in range(4):
-            own_gate[4 * k + i] = gates[i : i + 1]
-            far_gate[4 * k + i] = gates[4 + i : 5 + i]
-        both = jnp.concatenate([main, packed], axis=1).reshape(2, 4, LEAD, -1)
+        gates = jnp.sum(gate_m.reshape(2 * n, LEAD, 128), axis=1) + jnp.sum(
+            gate_r.reshape(2 * n, REST, 128), axis=1
+        )
+        for i in range(n):
+            own_gate[lo + i] = gates[i : i + 1]
+            far_gate[lo + i] = gates[n + i : n + i + 1]
+        both = jnp.concatenate([main, packed], axis=1).reshape(2, n, LEAD, -1)
         far_piece[span] = both[1]
         own_piece[span] = both[0]
-        piece_gate[k] = remote(
-            far_gate.at[pl.ds(4 * k, 4)], near_gate.at[pl.ds(4 * k, 4)],
-            s5.at[k], r5.at[k], (other, me),
-        )
-        piece_gate[k].start()
-        for i in range(4):
-            s = 4 * k + i
+        if lo >= DIRECT:
+            for s in range(lo, hi):
+                there, here = (other, peer(s)), (space, peer(s))
+                piece_copy[s] = remote(far_piece.at[s], near_in.at[s], s3.at[s], r3.at[s], there)
+                piece_copy[s].start()
+                far_gates[s] = remote(far_gate.at[s], near_gate.at[s], s5.at[s], r5.at[s], there)
+                far_gates[s].start()
+                if s == SELF:
+                    home[s] = own_piece[s]
+                    home_gate[s] = own_gate[s]
+                    continue
+                home_copy[s] = remote(own_piece.at[s], home.at[s], s4.at[s], r4.at[s], here)
+                home_copy[s].start()
+                home_gates[s] = remote(own_gate.at[s], home_gate.at[s], s6.at[s], r6.at[s], here)
+                home_gates[s].start()
+            return
+        piece_gate[c] = remote(
+            far_gate.at[pl.ds(lo, n)], near_gate.at[pl.ds(lo, n)],
+            s5.at[c], r5.at[c], (other, me),
+        )
+        piece_gate[c].start()
+        for s in range(lo, hi):
             piece_copy[s] = remote(
                 far_piece.at[s], near_in.at[s], s3.at[s], r3.at[s], (other, me)
             )
             piece_copy[s].start()
 
-    def finish(k):
-        piece_gate[k].wait_recv()
-        for i in range(4):
-            s = 4 * k + i
+    def finish(c):
+        piece_gate[c].wait_recv()
+        for s in range(*CHUNKS[c]):
             piece_copy[s].wait_recv()
             summed = (own_piece[s].astype(F32) + near_in[s].astype(F32)).astype(BF)
             gate = (own_gate[s] + near_gate[s]).astype(BF).astype(F32)
-            if s:
-                out_gate[s] = gate
-                home_gates[s] = remote(
-                    out_gate.at[s], home_gate.at[s], s6.at[s], r6.at[s], (space, origin(k, i))
-                )
-                home_gates[s].start()
-                home_out[s] = summed
-                home_copy[s] = remote(
-                    home_out.at[s], home.at[s], s4.at[s], r4.at[s], (space, origin(k, i))
-                )
-                home_copy[s].start()
-            else:
-                home[s] = summed
-                home_gate[s] = gate
+            out_gate[s] = gate
+            home_gates[s] = remote(
+                out_gate.at[s], home_gate.at[s], s6.at[s], r6.at[s], (space, peer(s))
+            )
+            home_gates[s].start()
+            home_out[s] = summed
+            home_copy[s] = remote(
+                home_out.at[s], home.at[s], s4.at[s], r4.at[s], (space, peer(s))
+            )
+            home_copy[s].start()
+
+    grad_w = 1024
 
     def first_tile(f, carry):
-        cols = pl.ds(pl.multiple_of(f * step_w, step_w), step_w)
+        cols = pl.ds(pl.multiple_of(f * grad_w, grad_w), grad_w)
         d_first[:, cols] = mm(x_all[...], pre_all[:, cols], 0, 0)
         return carry
 
     def second_tile(f, carry):
-        cols = pl.ds(pl.multiple_of(f * step_w, step_w), step_w)
+        cols = pl.ds(pl.multiple_of(f * grad_w, grad_w), grad_w)
         d_second[cols, :] = mm(act_all[:, cols], sc_all[...], 0, 0)
         return carry
 
-    for n in range(len(ORDER) + 2):
-        if n < len(ORDER):
-            arrive(ORDER[n])
-        if n == 1:
-            load1.wait()
-            load2.wait()
-        if 1 <= n < len(ORDER) + 1:
-            work(ORDER[n - 1])
-        if n == len(ORDER):
-            finish(ORDER[n - 2])
-            lax.fori_loop(0, hidden_n // step_w, first_tile, 0)
-        elif n >= 2:
-            finish(ORDER[n - 2])
-    lax.fori_loop(0, hidden_n // step_w, second_tile, 0)
-    for s in range(1, slots):
-        home_copy[s].wait_recv()
-        home_gates[s].wait_recv()
+    for s in FIRST:
+        relay(s)
+    self_copy.wait()
+    load1.wait()
+    load2.wait()
+    for c in range(len(CHUNKS)):
+        with mark("work%d" % c):
+            work(c)
+        if 0 < c and CHUNKS[c - 1][0] < DIRECT:
+            with mark("finish%d" % (c - 1)):
+                finish(c - 1)
+    with mark("first"):
+        lax.fori_loop(0, hidden_n // grad_w, first_tile, 0)
+    with mark("second"):
+        lax.fori_loop(0, hidden_n // grad_w, second_tile, 0)
+    with mark("homewait"):
+        for s in peers:
+            home_copy[s].wait_recv()
+            home_gates[s].wait_recv()
+        for s in range(DIRECT, slots):
+            piece_copy[s].wait_recv()
+            far_gates[s].wait_recv()
+    ends = slice(DIRECT, slots)
+    home[ends] = (home[ends].astype(F32) + near_in[ends].astype(F32)).astype(BF)
+    home_gate[ends] = (home_gate[ends] + near_gate[ends]).astype(BF).astype(F32)
 
     lead = home[:, :, 0:width].reshape(rows, width)
     packed = home[:, :, width : width + quarter_w].reshape(rows, quarter_w)
@@ -509,14 +555,16 @@
         d_gates[k : k + 1, :] = (row / gates_t[k : k + 1, :].astype(F32)).astype(BF)
 
     for s in range(slots):
-        if s:
+        if s != SELF:
             out_copy[s].wait_send()
             home_copy[s].wait_send()
             home_gates[s].wait_send()
         relay_copy[s].wait_send()
         piece_copy[s].wait_send()
-    for k in ORDER:
-        piece_gate[k].wait_send()
+    for s in range(DIRECT, slots):
+        far_gates[s].wait_send()
+    for c in piece_gate:
+        piece_gate[c].wait_send()
 
 
 def write_out(*refs):
@@ -533,6 +581,7 @@
     hidden_n = w_in.shape[2]
     slots = lax.axis_size("expert")
     rows = 2 * slots * (LEAD + REST)
+    most = max(hi - lo for lo, hi in CHUNKS)
     block_w = 2 * width + width // 2
     piece_w = width + width // 4
     vmem = pl.BlockSpec(memory_space=pltpu.VMEM)
@@ -565,7 +614,7 @@
             pltpu.VMEM((slots, LEAD, piece_w), BF),
             pltpu.VMEM((2, slots * LEAD, count), BF),
             pltpu.VMEM((2, slots * LEAD, count), BF),
-            pltpu.VMEM((8 * (LEAD + REST), width), F32),
+            pltpu.VMEM((2 * most * (LEAD + REST), width), F32),
             pltpu.VMEM((width, hidden_n), BF),
             pltpu.VMEM((hidden_n, width), BF),
             pltpu.VMEM((count, width), BF),

time: 47.3 us -> 45.1 us (0.953)
  Pallas kernels: 46.1 us -> 44.3 us
    pallas_call x1, Pallas kernels: 42.6 us -> 40.9 us  [on_device_fused(): pl.pallas_call(fused, out_shape=(shape((count, width), BF), shape((2, cou...]
where the time goes in v1:
time: 45.1 us; the launch traced here: 45 us
  Pallas kernels  44.3 us (98%)
  between operations  0.64 us (1%)
    pallas_call x1, Pallas kernels, on_device_fused(): pl.pallas_call(fused, out_shape=(shape((count, width), BF), shape((2, cou...  40.9 us
    pallas_call x1, Pallas kernels, on_device_fused(): pl.pallas_call(write_out, out_shape=tuple((shape(a.shape, a.dtype) for a...  3.48 us

profile of v1, /device:TPU:1, one launch (start us, length us, event | category | flops | bytes accessed | tf_op | source)
XLA Modules:
  0.0 45.0 jit_solution(13707038171815229382)
XLA Ops:
  0.6 40.9 %shard_map.102 = (bf16[128,512]{1,0:T(8,128)(2,1)S(1)}, bf16[2,128]{1,0:T(2,128)(2,1)S(1)}, f32[512,2048]{1,0:T(8,128)S(1)}, f32[2048,512]{1,0:T(8,128)S(1)}) custom-call(bf16[128,512]{1,0:T(8,128)(2,1)} %tiles_h.1, bf16[128,512]{1,0:T(8,128)(2,1)} %cotan_h.1, s32[1,128]{1,0:T(1,128)} %bitcast.7, s32[2,128]{1,0:T(2,128)} %bitcast.6, bf16[2,128]{1,0:T(2,128)(2,1)} %bitcast.8, ...), custom_call_target="tpu_custom_call" | custom-call | tf_op jit(solution)/shard_map/pallas_call | solution.py:592
  41.5 3.5 %shard_map.103 = (bf16[128,512]{1,0:T(8,128)(2,1)}, bf16[2,128]{1,0:T(2,128)(2,1)}, f32[512,2048]{1,0:T(8,128)}, f32[2048,512]{1,0:T(8,128)}) custom-call(bf16[128,512]{1,0:T(8,128)(2,1)S(1)} %get-tuple-element.12.refs_0_, bf16[2,128]{1,0:T(2,128)(2,1)S(1)} %get-tuple-element.13.refs_1_, f32[512,2048]{1,0:T(8,128)S(1)} %get-tuple-element.14.refs_2_, ...), custom_call_target="tpu_custom_call" | custom-call | tf_op jit(solution)/shard_map/pallas_call | solution.py:641

commit v2 on v1

--- a/solution.py
+++ b/solution.py
@@ -361,11 +361,11 @@
     self_copy = pltpu.make_async_copy(send.at[SELF], recv.at[0, SELF], sem_self)
     self_copy.start()
     relay_copy[SELF] = remote(
-        send.at[SELF], recv.at[1, SELF], s2.at[SELF], r2.at[SELF], (other, me)
+        send.at[SELF], recv.at[1, SELF], s2, r2.at[SELF // 4], (other, me)
     )
     relay_copy[SELF].start()
     for s in SENDS:
-        out_copy[s] = remote(send.at[s], recv.at[0, s], s1.at[s], r1.at[s], (space, peer(s)))
+        out_copy[s] = remote(send.at[s], recv.at[0, s], s1, r1.at[s], (space, peer(s)))
         out_copy[s].start()
 
     consts = {}
@@ -389,7 +389,7 @@
         with mark("arrive%d" % s):
             out_copy[s].wait_recv()
         relay_copy[s] = remote(
-            recv.at[0, s], recv.at[1, s], s2.at[s], r2.at[s], (other, me)
+            recv.at[0, s], recv.at[1, s], s2, r2.at[s // 4], (other, me)
         )
         relay_copy[s].start()
 
@@ -400,8 +400,8 @@
         chunk = block + rest
         spread_q, grow, pulls = consts[block]
         with mark("relayed%d" % c):
-            for s in range(lo, hi):
-                relay_copy[s].wait_recv()
+            both = recv.at[0, pl.ds(lo, n)], recv.at[1, pl.ds(lo, n)]
+            remote(*both, s2, r2.at[c], (other, me)).wait_recv()
         base = 2 * lo * (LEAD + REST)
         span = slice(lo, hi)
         x_all[base : base + block, :] = recv[:, span, :, 0:width].reshape(block, width)
@@ -460,44 +460,45 @@
         if lo >= DIRECT:
             for s in range(lo, hi):
                 there, here = (other, peer(s)), (space, peer(s))
-                piece_copy[s] = remote(far_piece.at[s], near_in.at[s], s3.at[s], r3.at[s], there)
+                piece_copy[s] = remote(far_piece.at[s], near_in.at[s], s3, r3.at[2], there)
                 piece_copy[s].start()
-                far_gates[s] = remote(far_gate.at[s], near_gate.at[s], s5.at[s], r5.at[s], there)
+                far_gates[s] = remote(far_gate.at[s], near_gate.at[s], s5, r5.at[2], there)
                 far_gates[s].start()
                 if s == SELF:
                     home[s] = own_piece[s]
                     home_gate[s] = own_gate[s]
                     continue
-                home_copy[s] = remote(own_piece.at[s], home.at[s], s4.at[s], r4.at[s], here)
+                home_copy[s] = remote(own_piece.at[s], home.at[s], s4, r4, here)
                 home_copy[s].start()
-                home_gates[s] = remote(own_gate.at[s], home_gate.at[s], s6.at[s], r6.at[s], here)
+                home_gates[s] = remote(own_gate.at[s], home_gate.at[s], s6, r6, here)
                 home_gates[s].start()
             return
         piece_gate[c] = remote(
             far_gate.at[pl.ds(lo, n)], near_gate.at[pl.ds(lo, n)],
-            s5.at[c], r5.at[c], (other, me),
+            s5, r5.at[c], (other, me),
         )
         piece_gate[c].start()
         for s in range(lo, hi):
             piece_copy[s] = remote(
-                far_piece.at[s], near_in.at[s], s3.at[s], r3.at[s], (other, me)
+                far_piece.at[s], near_in.at[s], s3, r3.at[c], (other, me)
             )
             piece_copy[s].start()
 
     def finish(c):
         piece_gate[c].wait_recv()
+        span = pl.ds(CHUNKS[c][0], CHUNKS[c][1] - CHUNKS[c][0])
+        remote(far_piece.at[span], near_in.at[span], s3, r3.at[c], (other, me)).wait_recv()
         for s in range(*CHUNKS[c]):
-            piece_copy[s].wait_recv()
             summed = (own_piece[s].astype(F32) + near_in[s].astype(F32)).astype(BF)
             gate = (own_gate[s] + near_gate[s]).astype(BF).astype(F32)
             out_gate[s] = gate
             home_gates[s] = remote(
-                out_gate.at[s], home_gate.at[s], s6.at[s], r6.at[s], (space, peer(s))
+                out_gate.at[s], home_gate.at[s], s6, r6, (space, peer(s))
             )
             home_gates[s].start()
             home_out[s] = summed
             home_copy[s] = remote(
-                home_out.at[s], home.at[s], s4.at[s], r4.at[s], (space, peer(s))
+                home_out.at[s], home.at[s], s4, r4, (space, peer(s))
             )
             home_copy[s].start()
 
@@ -528,13 +529,14 @@
         lax.fori_loop(0, hidden_n // grad_w, first_tile, 0)
     with mark("second"):
         lax.fori_loop(0, hidden_n // grad_w, second_tile, 0)
+    most, far = pl.ds(0, slots - 1), pl.ds(DIRECT, slots - DIRECT)
+    homes = remote(home_out.at[most], home.at[most], s4, r4, (other, me))
+    gates = remote(out_gate.at[most], home_gate.at[most], s6, r6, (other, me))
     with mark("homewait"):
-        for s in peers:
-            home_copy[s].wait_recv()
-            home_gates[s].wait_recv()
-        for s in range(DIRECT, slots):
-            piece_copy[s].wait_recv()
-            far_gates[s].wait_recv()
+        homes.wait_recv()
+        gates.wait_recv()
+        remote(far_piece.at[far], near_in.at[far], s3, r3.at[2], (other, me)).wait_recv()
+        remote(far_gate.at[far], near_gate.at[far], s5, r5.at[2], (other, me)).wait_recv()
     ends = slice(DIRECT, slots)
     home[ends] = (home[ends].astype(F32) + near_in[ends].astype(F32)).astype(BF)
     home_gate[ends] = (home_gate[ends] + near_gate[ends]).astype(BF).astype(F32)
@@ -554,17 +556,13 @@
         row = jnp.sum(jnp.where(iota((128, count), 0) == ranks[k], got, 0.0), axis=0, keepdims=True)
         d_gates[k : k + 1, :] = (row / gates_t[k : k + 1, :].astype(F32)).astype(BF)
 
-    for s in range(slots):
-        if s != SELF:
-            out_copy[s].wait_send()
-            home_copy[s].wait_send()
-            home_gates[s].wait_send()
-        relay_copy[s].wait_send()
-        piece_copy[s].wait_send()
-    for s in range(DIRECT, slots):
-        far_gates[s].wait_send()
-    for c in piece_gate:
-        piece_gate[c].wait_send()
+    with mark("sendwait"):
+        remote(send.at[most], recv.at[0, most], s1, r1.at[0], (other, me)).wait_send()
+        remote(recv.at[0], recv.at[1], s2, r2.at[0], (other, me)).wait_send()
+        remote(far_piece, near_in, s3, r3.at[0], (other, me)).wait_send()
+        remote(far_gate, near_gate, s5, r5.at[0], (other, me)).wait_send()
+        homes.wait_send()
+        gates.wait_send()
 
 
 def write_out(*refs):
@@ -625,7 +623,8 @@
             dma((7,)),
             dma(()),
         ]
-        + [dma((slots,))] * 12,
+        + [dma(()), dma((slots,)), dma(()), dma((4,)), dma(()), dma((3,)), dma(()), dma(())]
+        + [dma(()), dma((3,)), dma(()), dma(())],
         compiler_params=pltpu.CompilerParams(
             collective_id=0, has_side_effects=True, vmem_limit_bytes=36 * 1024 * 1024
         ),

time: 45.1 us -> 43.6 us (0.967)
  Pallas kernels: 44.3 us -> 42.8 us
    pallas_call x1, Pallas kernels: 40.9 us -> 39.3 us  [on_device_fused(): pl.pallas_call(fused, out_shape=(shape((count, width), BF), shape((2, cou...]
where the time goes in v2:
time: 43.6 us; the launch traced here: 43.4 us
  Pallas kernels  42.8 us (98%)
  between operations  0.64 us (1%)
    pallas_call x1, Pallas kernels, on_device_fused(): pl.pallas_call(fused, out_shape=(shape((count, width), BF), shape((2, cou...  39.3 us
    pallas_call x1, Pallas kernels, on_device_fused(): pl.pallas_call(write_out, out_shape=tuple((shape(a.shape, a.dtype) for a...  3.48 us

profile of v2, /device:TPU:1, one launch (start us, length us, event | category | flops | bytes accessed | tf_op | source)
XLA Modules:
  0.0 43.4 jit_solution(3629690404882419657)
XLA Ops:
  0.6 39.3 %shard_map.102 = (bf16[128,512]{1,0:T(8,128)(2,1)S(1)}, bf16[2,128]{1,0:T(2,128)(2,1)S(1)}, f32[512,2048]{1,0:T(8,128)S(1)}, f32[2048,512]{1,0:T(8,128)S(1)}) custom-call(bf16[128,512]{1,0:T(8,128)(2,1)} %tiles_h.1, bf16[128,512]{1,0:T(8,128)(2,1)} %cotan_h.1, s32[1,128]{1,0:T(1,128)} %bitcast.7, s32[2,128]{1,0:T(2,128)} %bitcast.6, bf16[2,128]{1,0:T(2,128)(2,1)} %bitcast.8, ...), custom_call_target="tpu_custom_call" | custom-call | tf_op jit(solution)/shard_map/pallas_call | solution.py:590
  39.9 3.5 %shard_map.103 = (bf16[128,512]{1,0:T(8,128)(2,1)}, bf16[2,128]{1,0:T(2,128)(2,1)}, f32[512,2048]{1,0:T(8,128)}, f32[2048,512]{1,0:T(8,128)}) custom-call(bf16[128,512]{1,0:T(8,128)(2,1)S(1)} %get-tuple-element.12.refs_0_, bf16[2,128]{1,0:T(2,128)(2,1)S(1)} %get-tuple-element.13.refs_1_, f32[512,2048]{1,0:T(8,128)S(1)} %get-tuple-element.14.refs_2_, ...), custom_call_target="tpu_custom_call" | custom-call | tf_op jit(solution)/shard_map/pallas_call | solution.py:640

commit v3 on v2

--- a/solution.py
+++ b/solution.py
@@ -201,6 +201,7 @@
 SELF = 12
 CHUNKS = ((0, 4), (4, 8), (8, 12), (12, 16))
 DIRECT = 8
+PARTS = 4
 SENDS = (13, 14, 15, 0, 1, 2, 3, 4, 5, 6, 7, 8, 9, 10, 11)
 FIRST = (13, 14, 0, 1, 2, 3, 15, 4)
 DURING = ((6, 5, 7), (8, 9, 10, 11), (), ())
@@ -278,9 +279,7 @@
 
     load1.start()
     load2.start()
-    with mark("small"):
-        for copy in small:
-            copy.wait()
+    small[0].wait()
     ids = ids_t[...]
     rel = ids ^ me
     near, plane = rel & 3, (rel >> 2) ^ (rel >> 3)
@@ -303,6 +302,7 @@
         pick_m[k] = (row_id == code_m).astype(F32).astype(BF)
         pick_t[k] = (row_tail == code_t).astype(F32).astype(BF)
 
+    small[1].wait()
     diagonal = iota((count, count), 0) == iota((count, count), 1)
     frame = jnp.sum(jnp.where(diagonal, frames_t[...].astype(F32), 0.0), axis=1, keepdims=True)
     frequency = (1 + lax.rem(iota((1, half), 1), 3)).astype(F32)
@@ -324,8 +324,11 @@
             [cos_v * u - sin_v * v, sin_v * u + cos_v * v], axis=1
         ).astype(BF)
 
+    small[3].wait()
     rotated = turn(tiles)
+    small[4].wait()
     turned = turn(cotan)
+    small[2].wait()
     g0 = gates_t[0:1, :].astype(F32)
     g1 = gates_t[1:2, :].astype(F32)
 
@@ -567,7 +570,14 @@
 
 def write_out(*refs):
     held, outs, sem = refs[:4], refs[4:8], refs[8]
-    copies = [pltpu.make_async_copy(held[n], outs[n], sem.at[n]) for n in range(4)]
+    copies = [pltpu.make_async_copy(held[n], outs[n], sem.at[n]) for n in range(2)]
+    for n in (2, 3):
+        part = held[n].shape[0] // PARTS
+        for p in range(PARTS):
+            rows = pl.ds(p * part, part)
+            copies.append(
+                pltpu.make_async_copy(held[n].at[rows], outs[n].at[rows], sem.at[len(copies)])
+            )
     for copy in copies:
         copy.start()
     for copy in copies:
@@ -642,7 +652,7 @@
         out_shape=tuple(shape(a.shape, a.dtype) for a in results),
         in_specs=[vmem] * 4,
         out_specs=[hbm] * 4,
-        scratch_shapes=[dma((4,))],
+        scratch_shapes=[dma((2 + 2 * PARTS,))],
         compiler_params=pltpu.CompilerParams(vmem_limit_bytes=4 * 1024 * 1024),
     )(*results)
     return (d_tiles, d_gates.T, d_first[None], d_second[None])

time: 43.6 us -> 43.5 us (level)
  no operation moved by 1% of the time
where the time goes in v3:
time: 43.5 us; the launch traced here: 43.4 us
  Pallas kernels  42.7 us (98%)
  between operations  0.64 us (1%)
    pallas_call x1, Pallas kernels, on_device_fused(): pl.pallas_call(fused, out_shape=(shape((count, width), BF), shape((2, cou...  39.3 us
    pallas_call x1, Pallas kernels, on_device_fused(): pl.pallas_call(write_out, out_shape=tuple((shape(a.shape, a.dtype) for a...  3.43 us

profile of v3, /device:TPU:1, one launch (start us, length us, event | category | flops | bytes accessed | tf_op | source)
XLA Modules:
  0.0 43.4 jit_solution(1030638187731538782)
XLA Ops:
  0.6 39.3 %shard_map.102 = (bf16[128,512]{1,0:T(8,128)(2,1)S(1)}, bf16[2,128]{1,0:T(2,128)(2,1)S(1)}, f32[512,2048]{1,0:T(8,128)S(1)}, f32[2048,512]{1,0:T(8,128)S(1)}) custom-call(bf16[128,512]{1,0:T(8,128)(2,1)} %tiles_h.1, bf16[128,512]{1,0:T(8,128)(2,1)} %cotan_h.1, s32[1,128]{1,0:T(1,128)} %bitcast.7, s32[2,128]{1,0:T(2,128)} %bitcast.6, bf16[2,128]{1,0:T(2,128)(2,1)} %bitcast.8, ...), custom_call_target="tpu_custom_call" | custom-call | tf_op jit(solution)/shard_map/pallas_call | solution.py:600
  39.9 3.4 %shard_map.103 = (bf16[128,512]{1,0:T(8,128)(2,1)}, bf16[2,128]{1,0:T(2,128)(2,1)}, f32[512,2048]{1,0:T(8,128)}, f32[2048,512]{1,0:T(8,128)}) custom-call(bf16[128,512]{1,0:T(8,128)(2,1)S(1)} %get-tuple-element.12.refs_0_, bf16[2,128]{1,0:T(2,128)(2,1)S(1)} %get-tuple-element.13.refs_1_, f32[512,2048]{1,0:T(8,128)S(1)} %get-tuple-element.14.refs_2_, ...), custom_call_target="tpu_custom_call" | custom-call | tf_op jit(solution)/shard_map/pallas_call | solution.py:650
